TPU v7x, 32 devices: a whole 2x2x4 slice. The times are simulated.
32 devices in a mesh: seq: 4 (over x, core), mp: 8 (over z, y).
Axes of the slice: x: 2, y: 2, z: 4, core: 2. Of those that a mesh axis runs over, the one named last changes fastest.
Arguments:
- tokens: bfloat16 [2, 6144, 1024], P(None, ('seq', 'mp')), may hold values from -6 to 6
- ln1_gain: float32 [1024], replicated, may hold values from 0.1 to 1.9
- ln1_bias: float32 [1024], replicated, may hold values from -1.75 to 1.75
- ln2_gain: float32 [1024], replicated, may hold values from 0.1 to 1.9
- ln2_bias: float32 [1024], replicated, may hold values from -1.75 to 1.75
- q_weight: bfloat16 [1024, 1024], P('seq', 'mp'), may hold values from -0.1875 to 0.1875
- k_weight: bfloat16 [1024, 1024], P('seq', 'mp'), may hold values from -0.1875 to 0.1875
- value_weight: bfloat16 [1024, 1024], P('seq', 'mp'), may hold values from -0.1875 to 0.1875
- out_weight: bfloat16 [1024, 1024], P('mp', 'seq'), may hold values from -2 to 2
- up_weight: bfloat16 [1024, 4096], P('seq', 'mp'), may hold values from -0.1875 to 0.1875
- down_weight: bfloat16 [4096, 1024], P('mp', 'seq'), may hold values from -0.09375 to 0.09375
- lengths: int32 [2, 4, 3], P(None, 'seq'), may hold values from 1 to 1024, 1536 in all within a row
- cotangent: bfloat16 [2, 6144, 1024], P(None, ('seq', 'mp')), may hold values from -12 to 12
Outputs:
- mixed: bfloat16 [2, 6144, 1024], P(None, ('seq', 'mp'))
- grad_tokens: float32 [2, 6144, 1024], P(None, ('seq', 'mp'))
- grad_ln1_gain: float32 [1024], replicated
- grad_ln1_bias: float32 [1024], replicated
- grad_ln2_gain: float32 [1024], replicated
- grad_ln2_bias: float32 [1024], replicated
- grad_q_weight: float32 [1024, 1024], P('seq', 'mp')
- grad_k_weight: float32 [1024, 1024], P('seq', 'mp')
- grad_v_weight: float32 [1024, 1024], P('seq', 'mp')
- grad_out_weight: float32 [1024, 1024], P('mp', 'seq')
- grad_up_weight: float32 [1024, 4096], P('seq', 'mp')
- grad_down_weight: float32 [4096, 1024], P('mp', 'seq')
Inputs may be any that keep to these rules, and one draw needn't show every extreme that they name: lengths[m, s] lists the 3 documents of row group s of micro-batch m in order; each row sums to 1536, and its longest document holds exactly 1024 tokens.
All inputs are finite; a program needn't handle non-finite values.
Results may differ from a plain program's by a relative error of at most 0.013.
Values may be sent and summed in bfloat16 or wider, within the bound.
No kernel may reach another device: no remote copies, remote signals or barrier semaphores. Data moves between devices by JAX's collectives and lax.ppermute only.
A program may use at most 192 MiB of HBM per device.

v0:
```python
from functools import partial
import math
import jax
import jax.numpy as jnp
from jax import lax
from jax.sharding import PartitionSpec as P

HEAD_DIM = 64
ROT = 16
FEATS = 64


def prime_list(wanted):
    found_primes = []
    candidate = 2
    while len(found_primes) < wanted:
        if all((candidate % earlier != 0 for earlier in found_primes)):
            found_primes.append(candidate)
        candidate += 1
    return found_primes


def feature_maps(head_width, feature_count):
    primes_found = prime_list(head_width)
    uniform_rows = [
        [
            min(max((row_idx + 0.5) * math.sqrt(prime_val) % 1.0, 0.001), 0.999)
            for prime_val in primes_found
        ]
        for row_idx in range(feature_count)
    ]
    uniform_pts = jnp.asarray(uniform_rows, jnp.float32)
    points = math.sqrt(2.0) * lax.erf_inv(2.0 * uniform_pts - 1.0)
    cosine_rows = [
        [
            math.sqrt(2.0 / head_width)
            * math.cos(math.pi * (cell_idx + 0.5) * freq_idx / head_width)
            * (math.sqrt(0.5) if freq_idx == 0 else 1.0)
            for cell_idx in range(head_width)
        ]
        for freq_idx in range(head_width)
    ]
    cosine = jnp.asarray(cosine_rows, jnp.float32)
    project = jnp.dot(points, cosine, precision=lax.Precision.HIGHEST)
    project = jnp.transpose(project) * (1.0 / math.sqrt(head_width))
    weighting = 1.0 / (1.0 + jnp.sum(points * points, axis=1) / head_width)
    return (project, weighting)


def rotate_heads(values, offset):
    half_dims = ROT // 2
    inverse = 10000.0 ** (-jnp.arange(half_dims, dtype=jnp.float32) * 2.0 / ROT)
    angles = offset[:, None] * inverse[None, :]
    cosine = jnp.cos(angles)[None, :, :]
    sine_part = jnp.sin(angles)[None, :, :]
    first_half = values[..., :half_dims]
    second = values[..., half_dims:ROT]
    return jnp.concatenate(
        [
            first_half * cosine - second * sine_part,
            second * cosine + first_half * sine_part,
            values[..., ROT:],
        ],
        axis=-1,
    )


def layer_norm(values, gain_vec, bias_vec):
    centered = values - jnp.mean(values, axis=-1, keepdims=True)
    variance = jnp.mean(centered * centered, axis=-1, keepdims=True)
    return centered * lax.rsqrt(variance + 1e-05) * gain_vec + bias_vec


def exact_gelu(values):
    return jax.nn.gelu(values, approximate=False)


def doc_layout(doc_lengths, number_of_tokens):
    doc_ends = jnp.cumsum(doc_lengths).astype(jnp.int32)
    starts = (doc_ends - doc_lengths).astype(jnp.int32)
    places = jnp.arange(number_of_tokens, dtype=jnp.int32)
    segment = jnp.sum((places[:, None] >= doc_ends[None, :]).astype(jnp.int32), axis=1).astype(
        jnp.int32
    )
    member = segment[:, None] == jnp.arange(doc_lengths.shape[0], dtype=jnp.int32)[None, :]
    offset = places - jnp.sum(jnp.where(member, starts[None, :], 0), axis=1).astype(jnp.int32)
    return (segment, offset.astype(jnp.float32))


def contract_rows(left_side, right_side):
    return lax.dot_general(
        left_side, right_side, (((0,), (0,)), ((), ())), preferred_element_type=jnp.float32
    )


def contract_cols(left_side, right_side):
    return lax.dot_general(
        left_side, right_side, (((1,), (1,)), ((), ())), preferred_element_type=jnp.float32
    )


def local_attention(plain_query_rows, key_raw, value_raw, segment, offset, project, weighting):
    maximal_precision_mode = lax.Precision.HIGHEST
    number_of_tokens = plain_query_rows.shape[0]
    head_count = plain_query_rows.shape[1] // HEAD_DIM

    def heads_first(values):
        return jnp.transpose(values.reshape(number_of_tokens, head_count, HEAD_DIM), (1, 0, 2))

    rot_query = rotate_heads(heads_first(plain_query_rows), offset)
    rot_key = rotate_heads(heads_first(key_raw), offset)
    value_heads = heads_first(value_raw)
    feat_query = (
        jnp.exp(jnp.einsum("htd,df->htf", rot_query, project, precision=maximal_precision_mode))
        * weighting
    )
    feat_key = jnp.exp(
        jnp.einsum("htd,df->htf", rot_key, project, precision=maximal_precision_mode)
    )
    rows_per_block = min(512, number_of_tokens)
    block_count = number_of_tokens // rows_per_block

    def split_blocks(values):
        return jnp.transpose(
            values.reshape((head_count, block_count, rows_per_block, values.shape[2])), (1, 0, 2, 3)
        )

    def block_step(carry, pieces):
        kv_state, totals, previous = carry
        block_of_queries, block_of_keys, value_block, block_segment = pieces
        places = jnp.arange(block_segment.shape[0], dtype=jnp.int32)
        attention_scores = jnp.einsum(
            "ugy,uky->ugk", block_of_queries, block_of_keys, precision=maximal_precision_mode
        )
        allowed = (places[:, None] >= places[None, :]) & (
            block_segment[:, None] == block_segment[None, :]
        )
        attention_scores = jnp.where(allowed[None, :, :], attention_scores, 0.0)
        numerator = jnp.einsum(
            "hqk,hkd->hqd", attention_scores, value_block, precision=maximal_precision_mode
        )
        denominator = jnp.sum(attention_scores, axis=2)
        carried_in = (block_segment == previous)[None, :]
        numerator = numerator + jnp.where(
            carried_in[:, :, None],
            jnp.einsum(
                "hqf,hfd->hqd", block_of_queries, kv_state, precision=maximal_precision_mode
            ),
            0.0,
        )
        denominator = denominator + jnp.where(
            carried_in,
            jnp.einsum("hqf,hf->hq", block_of_queries, totals, precision=maximal_precision_mode),
            0.0,
        )
        final_output = block_segment[-1]
        carried_over = final_output == previous
        trailing_mask = (block_segment == final_output).astype(jnp.float32)
        new_state = jnp.where(carried_over, kv_state, 0.0) + jnp.einsum(
            "hrf,hrd,r->hfd",
            block_of_keys,
            value_block,
            trailing_mask,
            precision=maximal_precision_mode,
        )
        new_totals = jnp.where(carried_over, totals, 0.0) + jnp.einsum(
            "hrf,r->hf", block_of_keys, trailing_mask, precision=maximal_precision_mode
        )
        return ((new_state, new_totals, final_output), numerator / denominator[:, :, None])

    start_carry = (
        jnp.zeros((head_count, FEATS, HEAD_DIM), jnp.float32),
        jnp.zeros((head_count, FEATS), jnp.float32),
        jnp.array(-1, jnp.int32),
    )
    _, outputs = lax.scan(
        jax.checkpoint(block_step),
        start_carry,
        (
            split_blocks(feat_query),
            split_blocks(feat_key),
            split_blocks(value_heads),
            segment.reshape(block_count, rows_per_block),
        ),
    )
    joined = jnp.transpose(outputs, (1, 0, 2, 3)).reshape(head_count, number_of_tokens, HEAD_DIM)
    return jnp.transpose(joined, (1, 0, 2)).reshape(number_of_tokens, head_count * HEAD_DIM)


def local(
    tokens,
    ln1_gain,
    ln1_bias,
    ln2_gain,
    ln2_bias,
    q_weight,
    k_weight,
    value_weight,
    out_weight,
    up_weight,
    down_weight,
    lengths,
    cotangent,
):
    micro_count = tokens.shape[0]
    local_rows = tokens.shape[1]
    group_rows = local_rows * lax.axis_size("mp")
    seq_count = lax.axis_size("seq")
    project, weighting = feature_maps(HEAD_DIM, FEATS)
    grad_sums = [
        jnp.zeros((q_weight.shape[0] * seq_count, q_weight.shape[1]), jnp.float32),
        jnp.zeros((k_weight.shape[0] * seq_count, k_weight.shape[1]), jnp.float32),
        jnp.zeros((value_weight.shape[0] * seq_count, value_weight.shape[1]), jnp.float32),
        jnp.zeros((out_weight.shape[0], out_weight.shape[1] * seq_count), jnp.float32),
        jnp.zeros((up_weight.shape[0] * seq_count, up_weight.shape[1]), jnp.float32),
        jnp.zeros((down_weight.shape[0], down_weight.shape[1] * seq_count), jnp.float32),
    ]
    norm_sums = [
        jnp.zeros_like(ln1_gain),
        jnp.zeros_like(ln1_bias),
        jnp.zeros_like(ln2_gain),
        jnp.zeros_like(ln2_bias),
    ]
    mixed_parts = []
    grad_parts = []
    for micro_step in range(micro_count):
        full_weights = (
            lax.all_gather(q_weight, "seq", axis=0, tiled=True),
            lax.all_gather(k_weight, "seq", axis=0, tiled=True),
            lax.all_gather(value_weight, "seq", axis=0, tiled=True),
            lax.all_gather(out_weight, "seq", axis=1, tiled=True),
            lax.all_gather(up_weight, "seq", axis=0, tiled=True),
            lax.all_gather(down_weight, "seq", axis=1, tiled=True),
        )
        w_query, w_key, w_value, w_out, w_up, w_down = full_weights
        rows_in = tokens[micro_step].astype(jnp.float32)
        normed_one, pull_one = jax.vjp(layer_norm, rows_in, ln1_gain, ln1_bias)
        normed_two, pull_two = jax.vjp(layer_norm, rows_in, ln2_gain, ln2_bias)
        group_one, group_two = (
            lax.all_gather(normed_one.astype(jnp.bfloat16), "mp", axis=0, tiled=True),
            lax.all_gather(normed_two.astype(jnp.bfloat16), "mp", axis=0, tiled=True),
        )
        plain_query_rows = jnp.dot(group_one, w_query, preferred_element_type=jnp.float32)
        key_raw = jnp.dot(group_one, w_key, preferred_element_type=jnp.float32)
        value_raw = jnp.dot(group_one, w_value, preferred_element_type=jnp.float32)
        segment, offset = doc_layout(lengths[micro_step, 0], group_rows)
        attend = partial(
            local_attention, segment=segment, offset=offset, project=project, weighting=weighting
        )
        context, pull_attn = jax.vjp(attend, plain_query_rows, key_raw, value_raw)
        context_low = context.astype(jnp.bfloat16)
        hidden = jnp.dot(group_two, w_up, preferred_element_type=jnp.float32)
        activated, pull_gelu = jax.vjp(exact_gelu, hidden)
        activated_low = activated.astype(jnp.bfloat16)
        context_rows = lax.slice_in_dim(context_low, 0, lax.axis_size("mp") * local_rows, axis=0)
        active_rows = lax.slice_in_dim(activated_low, 0, lax.axis_size("mp") * local_rows, axis=0)
        branch_sum = lax.psum_scatter(
            jnp.dot(context_rows, w_out, preferred_element_type=jnp.float32)
            + jnp.dot(active_rows, w_down, preferred_element_type=jnp.float32),
            "mp",
            scatter_dimension=0,
            tiled=True,
        )
        mixed_parts.append((rows_in + branch_sum).astype(jnp.bfloat16))
        grad_group = lax.all_gather(cotangent[micro_step], "mp", axis=0, tiled=True)
        grad_context = contract_cols(grad_group, w_out)
        grad_activated = contract_cols(grad_group, w_down)
        grad_hidden = pull_gelu(grad_activated)[0].astype(jnp.bfloat16)
        grad_query_f, grad_key_f, grad_value_f = pull_attn(grad_context)
        grad_query = grad_query_f.astype(jnp.bfloat16)
        grad_key = grad_key_f.astype(jnp.bfloat16)
        grad_value = grad_value_f.astype(jnp.bfloat16)
        micro_grads = (
            contract_rows(group_one, grad_query),
            contract_rows(group_one, grad_key),
            contract_rows(group_one, grad_value),
            contract_rows(context_low, grad_group),
            contract_rows(group_two, grad_hidden),
            contract_rows(activated_low, grad_group),
        )
        grad_sums = [total + term for total, term in zip(grad_sums, micro_grads)]
        part_one = (
            contract_cols(grad_query, w_query)
            + contract_cols(grad_key, w_key)
            + contract_cols(grad_value, w_value)
        )
        part_two = contract_cols(grad_hidden, w_up)
        sum_one, sum_two = (
            lax.psum_scatter(
                part_one.astype(jnp.bfloat16), "mp", scatter_dimension=0, tiled=True
            ).astype(jnp.float32),
            lax.psum_scatter(
                part_two.astype(jnp.bfloat16), "mp", scatter_dimension=0, tiled=True
            ).astype(jnp.float32),
        )
        grad_in_one, grad_gain_one, grad_bias_one = pull_one(sum_one)
        grad_in_two, grad_gain_two, grad_bias_two = pull_two(sum_two)
        grad_parts.append(cotangent[micro_step].astype(jnp.float32) + grad_in_one + grad_in_two)
        norm_sums = [
            norm_sums[0] + grad_gain_one,
            norm_sums[1] + grad_bias_one,
            norm_sums[2] + grad_gain_two,
            norm_sums[3] + grad_bias_two,
        ]
    weight_grads = (
        lax.psum_scatter(
            grad_sums[0].astype(jnp.bfloat16), "seq", scatter_dimension=0, tiled=True
        ).astype(jnp.float32),
        lax.psum_scatter(
            grad_sums[1].astype(jnp.bfloat16), "seq", scatter_dimension=0, tiled=True
        ).astype(jnp.float32),
        lax.psum_scatter(
            grad_sums[2].astype(jnp.bfloat16), "seq", scatter_dimension=0, tiled=True
        ).astype(jnp.float32),
        lax.psum_scatter(
            grad_sums[3].astype(jnp.bfloat16), "seq", scatter_dimension=1, tiled=True
        ).astype(jnp.float32),
        lax.psum_scatter(
            grad_sums[4].astype(jnp.bfloat16), "seq", scatter_dimension=0, tiled=True
        ).astype(jnp.float32),
        lax.psum_scatter(
            grad_sums[5].astype(jnp.bfloat16), "seq", scatter_dimension=1, tiled=True
        ).astype(jnp.float32),
    )
    norm_grads = lax.psum((norm_sums[0], norm_sums[1], norm_sums[2], norm_sums[3]), ("seq", "mp"))
    return (
        jnp.stack(mixed_parts),
        jnp.stack(grad_parts),
        norm_grads[0],
        norm_grads[1],
        norm_grads[2],
        norm_grads[3],
        weight_grads[0],
        weight_grads[1],
        weight_grads[2],
        weight_grads[3],
        weight_grads[4],
        weight_grads[5],
    )


def solution(mesh):
    in_specs = (
        P(None, ("seq", "mp"), None),
        P(),
        P(),
        P(),
        P(),
        P("seq", "mp"),
        P("seq", "mp"),
        P("seq", "mp"),
        P("mp", "seq"),
        P("seq", "mp"),
        P("mp", "seq"),
        P(None, "seq", None),
        P(None, ("seq", "mp"), None),
    )
    out_specs = (
        P(None, ("seq", "mp"), None),
        P(None, ("seq", "mp"), None),
        P(),
        P(),
        P(),
        P(),
        P("seq", "mp"),
        P("seq", "mp"),
        P("seq", "mp"),
        P("mp", "seq"),
        P("seq", "mp"),
        P("mp", "seq"),
    )
    return jax.shard_map(local, mesh=mesh, in_specs=in_specs, out_specs=out_specs, check_vma=False)
```

profile of v0, /device:TPU:0, one launch (start us, length us, event | category | flops | bytes accessed | tf_op | source)
XLA Modules:
  0.0 1165.4 jit_solution(13924311496966079492)
XLA Ops:
  20.3 7.7 all_gather.43
  27.9 5.8 all_gather.45
  35.7 5.9 all_gather.44
  41.5 6.3 all_gather.46
  48.9 27.5 %all-gather.19.cloned.1.call-done = bf16[1536,1024]{1,0:T(8,128)(2,1)} async-done(((bf16[192,1024]{1,0:T(8,128)(2,1)}), bf16[1536,1024]{1,0:T(8,128)(2,1)}) %all-gather.19.cloned.1.call-update) | async-done | bytes 3145744 | tf_op jit(solution)/shard_map/all_gather | solution.py:240
  81.2 56.1 %all-gather.11.cloned.1.call-done = bf16[1536,1024]{1,0:T(8,128)(2,1)} async-done(((bf16[192,1024]{1,0:T(8,128)(2,1)}), bf16[1536,1024]{1,0:T(8,128)(2,1)}) %all-gather.11.cloned.1.call-update) | async-done | bytes 3145744 | tf_op jit(solution)/shard_map/all_gather | solution.py:240
  170.9 50.6 %while.95 = (s32[]{:T(128)}, f32[2,64,64]{2,1,0:T(8,128)S(1)}, f32[2,64]{1,0:T(2,128)S(1)}, s32[]{:T(128)}, bf16[3,2,512,64]{2,3,1,0:T(8,128)(2,1)}, /*index=5*/...) while((s32[]{:T(128)}, f32[2,64,64]{2,1,0:T(8,128)S(1)}, ...), condition=%wide.region_17.18_spmd.clone, body=%wide.region_15.17_spmd.clone.sunk | while | flops 910208896 | bytes 8145129 | solution.py:176
  194.8 3.3 fusion.628
  211.7 3.3 fusion.628
  228.2 79.3 %while.97 = (s32[]{:T(128)}, f32[2,64,64]{2,1,0:T(8,128)}, f32[2,64]{1,0:T(2,128)S(1)}, f32[3,2,512,64]{2,3,1,0:T(8,128)}, f32[3,2,512,64]{2,3,1,0:T(8,128)}, /*...) while((s32[]{:T(128)}, f32[2,64,64]{2,1,0:T(8,128)}, ...), condition=%wide.region_32.33_spmd.clone, body=%wide.region_29.32_spmd.clone.sunk | while | flops 2675472384 | bytes 24581376 | solution.py:176
  332.6 42.4 %while.94 = (s32[]{:T(128)}, f32[2,64,64]{2,1,0:T(8,128)S(1)}, f32[2,64]{1,0:T(2,128)S(1)}, s32[]{:T(128)}, bf16[3,2,512,64]{2,3,1,0:T(8,128)(2,1)}, /*index=5*/...) while((s32[]{:T(128)}, f32[2,64,64]{2,1,0:T(8,128)S(1)}, ...), condition=%wide.region_8.9_spmd.clone, body=%wide.region_6.8_spmd.clone.sunk | while | flops 910208896 | bytes 8145645 | solution.py:176
  337.9 3.3 fusion.613
  352.0 3.3 fusion.613
  366.2 3.3 fusion.613
  380.6 67.8 %while.96 = (s32[]{:T(128)}, f32[2,64,64]{2,1,0:T(8,128)S(1)}, f32[2,64]{1,0:T(2,128)S(1)}, f32[3,2,512,64]{2,3,1,0:T(8,128)}, f32[3,2,512,64]{2,3,1,0:T(8,128)}...) while((s32[]{:T(128)}, f32[2,64,64]{2,1,0:T(8,128)S(1)}, ...), condition=%wide.region_22.23_spmd.clone, body=%wide.region_19.22_spmd.clone.sunk | while | flops 2675472384 | bytes 24581376 | solution.py:176
  477.8 12.2 %multiply_convert_fusion.1 = (bf16[1536,512]{1,0:T(8,128)(2,1)}, f32[1536,512]{1,0:T(8,128)}, f32[1536,512]{1,0:T(8,128)}) fusion(bf16[1536,1024]{1,0:T(8,128)(2,1)} %all-gather.13.cloned.1.call-done, bf16[1024,512]{1,0:T(8,128)(2,1)} %all-gather.15.cloned.1.call-done), kind=kOutput, calls=%fused_computation.309 | convolution fusion | flops 1661730816 | bytes 12058624 | tf_op jit(solution)/shard_map/dot_general | solution.py:252
  490.0 12.0 %multiply_convert_fusion = (bf16[1536,512]{1,0:T(8,128)(2,1)}, f32[1536,512]{1,0:T(8,128)}, f32[1536,512]{1,0:T(8,128)}) fusion(bf16[1536,1024]{1,0:T(8,128)(2,1)} %all-gather.21.cloned.1.call-done, bf16[1024,512]{1,0:T(8,128)(2,1)} %all-gather.15.cloned.1.call-done), kind=kOutput, calls=%fused_computation.296 | convolution fusion | flops 1661730816 | bytes 12058624 | tf_op jit(solution)/shard_map/dot_general | solution.py:252
  502.0 6.1 add_convert_fusion.3
  519.9 4.3 fusion.234
  540.5 3.5 convolution_convert_fusion.1
  545.4 3.5 convolution_convert_fusion
  552.5 3.7 convolution_add_fusion.8
  559.6 3.8 convolution_add_fusion.9
  569.5 5.3 reduce-scatter.33.cloned.1.call-done
  576.6 25.4 %reduce-scatter.35.cloned.1.call-done = bf16[512,256]{1,0:T(8,128)(2,1)} async-done(((bf16[512,1024]{1,0:T(8,128)(2,1)}), bf16[512,256]{1,0:T(8,128)(2,1)}) %reduce-scatter.35.cloned.1.call-update) | async-done | bytes 262160 | tf_op jit(solution)/shard_map/reduce_scatter | solution.py:321
  603.8 76.1 %reduce-scatter.21.cloned.1.call-done = bf16[192,1024]{1,0:T(8,128)(2,1)} async-done(((bf16[1536,1024]{1,0:T(8,128)(2,1)}), bf16[192,1024]{1,0:T(8,128)(2,1)}) %reduce-scatter.21.cloned.1.call-update) | async-done | bytes 393232 | tf_op jit(solution)/shard_map/reduce_scatter | solution.py:289
  679.9 77.0 %reduce-scatter.17.cloned.1.call-done = bf16[192,1024]{1,0:T(8,128)(2,1)} async-done(((bf16[1536,1024]{1,0:T(8,128)(2,1)}), bf16[192,1024]{1,0:T(8,128)(2,1)}) %reduce-scatter.17.cloned.1.call-update) | async-done | bytes 393232 | tf_op jit(solution)/shard_map/reduce_scatter | solution.py:289
  758.5 75.5 %reduce-scatter.19.cloned.1.call-done = bf16[192,1024]{1,0:T(8,128)(2,1)} async-done(((bf16[1536,1024]{1,0:T(8,128)(2,1)}), bf16[192,1024]{1,0:T(8,128)(2,1)}) %reduce-scatter.19.cloned.1.call-update) | async-done | bytes 393232 | tf_op jit(solution)/shard_map/reduce_scatter | solution.py:292
  834.0 77.2 %reduce-scatter.23.cloned.1.call-done = bf16[192,1024]{1,0:T(8,128)(2,1)} async-done(((bf16[1536,1024]{1,0:T(8,128)(2,1)}), bf16[192,1024]{1,0:T(8,128)(2,1)}) %reduce-scatter.23.cloned.1.call-update) | async-done | bytes 393232 | tf_op jit(solution)/shard_map/reduce_scatter | solution.py:292
  916.1 43.2 %all-reduce.12 = (f32[1024]{0:T(1024)}, f32[1024]{0:T(1024)}, f32[1024]{0:T(1024)}, f32[1024]{0:T(1024)}) all-reduce(f32[1024]{0:T(1024)S(1)} %add.341, f32[1024]{0:T(1024)S(1)} %add.342, f32[1024]{0:T(1024)S(1)} %add.343, f32[1024]{0:T(1024)S(1)} %add.344), channel_id=1, replica_groups=mesh['seq'=4,'mp'=8] {'seq','mp'}, use_global_device_ids=true, to_apply=%region_41.42 | all-reduce | flops 4096 | bytes 32768 | tf_op jit(solution)/shard_map/psum | solution.py:325
  961.0 72.1 %reduce-scatter.15.cloned.1.call-done = f32[192,1024]{1,0:T(8,128)} async-done(((f32[1536,1024]{1,0:T(8,128)}), f32[192,1024]{1,0:T(8,128)}) %reduce-scatter.15.cloned.1.call-update) | async-done | bytes 786448 | tf_op jit(solution)/shard_map/reduce_scatter | solution.py:257
  1033.0 120.7 %reduce-scatter.13.cloned.1.call-done = f32[192,1024]{1,0:T(8,128)} async-done(((f32[1536,1024]{1,0:T(8,128)}), f32[192,1024]{1,0:T(8,128)}) %reduce-scatter.13.cloned.1.call-update) | async-done | bytes 786448 | tf_op jit(solution)/shard_map/reduce_scatter | solution.py:257
  (664 shorter events, 384.2 us)
Async XLA Ops:
  7.2 69.2 %all-gather.19.cloned.1.call-start = ((), (), s32[]{:S(2)}) async-start(), calls=%async_computation.17 | async-start | bytes 3538944 | tf_op jit(solution)/shard_map/all_gather | solution.py:240
  13.5 123.8 %all-gather.11.cloned.1.call-start = ((), (), s32[]{:S(2)}) async-start(), calls=%async_computation.12 | async-start | bytes 3538944 | tf_op jit(solution)/shard_map/all_gather | solution.py:240
  14.2 207.2 %all-gather.25.cloned.1.call-start = ((), (), s32[]{:S(2)}) async-start(), calls=%async_computation.31 | async-start | bytes 3538944 | tf_op jit(solution)/shard_map/all_gather | solution.py:265
  15.3 359.6 %all-gather.23.cloned.1.call-start = ((), (), s32[]{:S(2)}) async-start(), calls=%async_computation.30 | async-start | bytes 3538944 | tf_op jit(solution)/shard_map/all_gather | solution.py:265
  15.9 461.9 %all-gather.15.cloned.1.call-start = ((), (), s32[]{:S(2)}) async-start(), calls=%async_computation.14 | async-start | bytes 1310720 | tf_op jit(solution)/shard_map/all_gather | solution.py:232
  16.5 461.3 %all-gather.13.cloned.1.call-start = ((), (), s32[]{:S(2)}) async-start(), calls=%async_computation.13 | async-start | bytes 3538944 | tf_op jit(solution)/shard_map/all_gather | solution.py:241
  17.1 472.9 %all-gather.21.cloned.1.call-start = ((), (), s32[]{:S(2)}) async-start(), calls=%async_computation.18 | async-start | bytes 3538944 | tf_op jit(solution)/shard_map/all_gather | solution.py:241
  17.8 484.2 %all-gather.17.cloned.1.call-start = ((), (), s32[]{:S(2)}) async-start(), calls=%async_computation.15 | async-start | bytes 1310720 | tf_op jit(solution)/shard_map/all_gather | solution.py:233
  18.6 544.8 %reduce-scatter.27.cloned.1.call-start = ((), (), s32[]{:S(2)}) async-start(), calls=%async_computation.25 | async-start | bytes 327680 | tf_op jit(solution)/shard_map/reduce_scatter | solution.py:309
  41.5 285.3 %copy-start.18 = (bf16[1024,128]{1,0:T(8,128)(2,1)}, bf16[1024,128]{1,0:T(8,128)(2,1)S(1)}, u32[]{:S(2)}) copy-start(bf16[1024,128]{1,0:T(8,128)(2,1)S(1)} %all_gather.44) | copy-start | bytes 786436
  461.0 104.0 %reduce-scatter.25.cloned.1.call-start = ((), (), s32[]{:S(2)}) async-start(), calls=%async_computation.24 | async-start | bytes 327680 | tf_op jit(solution)/shard_map/reduce_scatter | solution.py:306
  468.6 97.9 %reduce-scatter.29.cloned.1.call-start = ((), (), s32[]{:S(2)}) async-start(), calls=%async_computation.26 | async-start | bytes 327680 | tf_op jit(solution)/shard_map/reduce_scatter | solution.py:312
  473.4 94.6 %reduce-scatter.31.cloned.1.call-start = ((), (), s32[]{:S(2)}) async-start(), calls=%async_computation.27 | async-start | bytes 327680 | tf_op jit(solution)/shard_map/reduce_scatter | solution.py:315
  477.7 97.1 %reduce-scatter.33.cloned.1.call-start = ((), (), s32[]{:S(2)}) async-start(), calls=%async_computation.28 | async-start | bytes 1310720 | tf_op jit(solution)/shard_map/reduce_scatter | solution.py:318
  519.8 82.3 %reduce-scatter.35.cloned.1.call-start = ((), (), s32[]{:S(2)}) async-start(), calls=%async_computation.29 | async-start | bytes 1310720 | tf_op jit(solution)/shard_map/reduce_scatter | solution.py:321
  527.0 152.9 %reduce-scatter.21.cloned.1.call-start = ((), (), s32[]{:S(2)}) async-start(), calls=%async_computation.22 | async-start | bytes 3538944 | tf_op jit(solution)/shard_map/reduce_scatter | solution.py:289
  533.1 223.8 %reduce-scatter.17.cloned.1.call-start = ((), (), s32[]{:S(2)}) async-start(), calls=%async_computation.20 | async-start | bytes 3538944 | tf_op jit(solution)/shard_map/reduce_scatter | solution.py:289
  538.8 295.2 %reduce-scatter.19.cloned.1.call-start = ((), (), s32[]{:S(2)}) async-start(), calls=%async_computation.21 | async-start | bytes 3538944 | tf_op jit(solution)/shard_map/reduce_scatter | solution.py:292
  544.0 367.3 %reduce-scatter.23.cloned.1.call-start = ((), (), s32[]{:S(2)}) async-start(), calls=%async_computation.23 | async-start | bytes 3538944 | tf_op jit(solution)/shard_map/reduce_scatter | solution.py:292
  549.0 484.1 %reduce-scatter.15.cloned.1.call-start = ((), (), s32[]{:S(2)}) async-start(), calls=%async_computation.19 | async-start | bytes 7077888 | tf_op jit(solution)/shard_map/reduce_scatter | solution.py:257
  556.2 597.6 %reduce-scatter.13.cloned.1.call-start = ((), (), s32[]{:S(2)}) async-start(), calls=%async_computation.16 | async-start | bytes 7077888 | tf_op jit(solution)/shard_map/reduce_scatter | solution.py:257
  563.3 193.6 %copy-start.73 = (f32[1024]{0:T(1024)S(1)}, f32[1024]{0:T(1024)}, u32[]{:S(2)}) copy-start(f32[1024]{0:T(1024)} %param.24) | copy-start | bytes 12292
  563.3 193.6 %copy-start.79 = (f32[192]{0:T(256)S(1)}, f32[192]{0:T(256)}, u32[]{:S(2)}) copy-start(f32[192]{0:T(256)} %copy-done.78) | copy-start | bytes 2308
  563.3 193.6 %copy-start.81 = (f32[192]{0:T(256)S(1)}, f32[192]{0:T(256)}, u32[]{:S(2)}) copy-start(f32[192]{0:T(256)} %copy-done.80) | copy-start | bytes 2308
  563.3 195.1 %copy-start.92 = (f32[192]{0:T(256)S(1)}, f32[192]{0:T(256)}, u32[]{:S(2)}) copy-start(f32[192]{0:T(256)} %copy-done.91) | copy-start | bytes 2308
  563.4 195.1 %copy-start.90 = (f32[192]{0:T(256)S(1)}, f32[192]{0:T(256)}, u32[]{:S(2)}) copy-start(f32[192]{0:T(256)} %copy-done.89) | copy-start | bytes 2308
  563.4 347.9 %copy-start.72 = (f32[1024]{0:T(1024)S(1)}, f32[1024]{0:T(1024)}, u32[]{:S(2)}) copy-start(f32[1024]{0:T(1024)} %param.26) | copy-start | bytes 12292
  563.4 347.9 %copy-start.83 = (f32[192]{0:T(256)S(1)}, f32[192]{0:T(256)}, u32[]{:S(2)}) copy-start(f32[192]{0:T(256)} %copy-done.82) | copy-start | bytes 2308
  563.4 347.9 %copy-start.88 = (f32[192]{0:T(256)S(1)}, f32[192]{0:T(256)}, u32[]{:S(2)}) copy-start(f32[192]{0:T(256)} %copy-done.87) | copy-start | bytes 2308
  679.9 279.5 %copy-start.36 = (bf16[192,1024]{1,0:T(8,128)(2,1)S(1)}, bf16[192,1024]{1,0:T(8,128)(2,1)}, u32[]{:S(2)}) copy-start(bf16[192,1024]{1,0:T(8,128)(2,1)} %reduce-scatter.21.cloned.1.call-done) | copy-start | bytes 1179652
  911.3 242.5 %copy-start.39 = (bf16[192,1024]{1,0:T(8,128)(2,1)S(1)}, bf16[192,1024]{1,0:T(8,128)(2,1)}, u32[]{:S(2)}) copy-start(bf16[192,1024]{1,0:T(8,128)(2,1)} %reduce-scatter.17.cloned.1.call-done) | copy-start | bytes 1179652
  911.3 242.5 %copy-start.40 = (bf16[192,1024]{1,0:T(8,128)(2,1)S(1)}, bf16[192,1024]{1,0:T(8,128)(2,1)}, u32[]{:S(2)}) copy-start(bf16[192,1024]{1,0:T(8,128)(2,1)} %reduce-scatter.19.cloned.1.call-done) | copy-start | bytes 1179652
  (99 other events, 983.0 us)
Sparse Core Ops, SparseCore 0:
  13.6 62.7 all-gather.18
  78.5 58.6 all-gather.10
  139.4 58.6 all-gather.24
  200.2 58.6 all-gather.22
  260.3 15.3 all-gather.14
  277.8 60.0 all-gather.12
  340.1 58.7 all-gather.20
  400.4 15.5 all-gather.16
  461.1 18.9 reduce-scatter.26
  482.4 20.0 reduce-scatter.24
  505.0 20.0 reduce-scatter.28
  527.4 20.0 reduce-scatter.30
  550.0 24.7 reduce-scatter.32
  577.2 24.7 reduce-scatter.34
  605.5 74.3 reduce-scatter.20
  683.3 73.4 reduce-scatter.16
  760.3 73.6 reduce-scatter.18
  837.5 73.7 reduce-scatter.22
  914.8 118.1 reduce-scatter.14
  1036.5 117.2 reduce-scatter.12
where the time goes:
time: 1180 us; the launch traced here: 1170 us
  waiting for transfers between devices  617 us (52%)
  matrix products  282 us (24%)
  local copies, waits for them, and re-layouts  104 us (9%)
  blocking collectives  68.9 us (6%)
  other arithmetic  58.9 us (5%)
  loops' own time  17.9 us (2%)
  between operations  16.3 us (1%)
    reduce_scatter x2, waiting for transfers between devices, local(): lax.psum_scatter(jnp.dot(context_rows, w_out, preferred_element_type=jnp....  193 us
    reduce_scatter x2, waiting for transfers between devices, local(): lax.psum_scatter(part_one.astype(jnp.bfloat16), 'mp', scatter_dimension=0...  153 us
    reduce_scatter x2, waiting for transfers between devices, local(): lax.psum_scatter(part_two.astype(jnp.bfloat16), 'mp', scatter_dimension=0...  153 us
    all_gather x2, waiting for transfers between devices, local(): lax.all_gather(normed_one.astype(jnp.bfloat16), 'mp', axis=0, tiled=True)  83.5 us
    dot_general x24, matrix products, block_step(): jnp.einsum('ugy,uky->ugk', block_of_queries, block_of_keys, precision=max...  55 us
    dot_general x24, matrix products, block_step(): jnp.einsum('hqk,hkd->hqd', attention_scores, value_block, precision=maxim...  54.8 us
    psum x1, blocking collectives, local(): lax.psum((norm_sums[0], norm_sums[1], norm_sums[2], norm_sums[3]), ('seq'...  43.2 us
    dot_general x12, matrix products, contract_cols(): lax.dot_general(left_side, right_side, (((1,), (1,)), ((), ())), preferre...  32.5 us
  transfers between devices with their start and end apart: 20, of which 10 were waited for; matrix products, arithmetic and copies ran while one was open for 36% of the time, Pallas kernels for 0%

commit v1 on v0

--- a/solution.py
+++ b/solution.py
@@ -236,8 +236,26 @@
         rows_in = tokens[micro_step].astype(jnp.float32)
         normed_one, pull_one = jax.vjp(layer_norm, rows_in, ln1_gain, ln1_bias)
         normed_two, pull_two = jax.vjp(layer_norm, rows_in, ln2_gain, ln2_bias)
+
+        def see_routes_all(mat):
+            named_axis = "mp"
+            f_now = jax.lax.axis_size(named_axis)
+            near, res = (f_now, jax.lax.axis_index(named_axis))
+            carry_out, current_arr = (mat, 1)
+            while current_arr < near:
+                heard = jax.lax.ppermute(
+                    carry_out,
+                    axis_name=named_axis,
+                    perm=list(map(lambda k: (k, k ^ current_arr), range(near))),
+                )
+                h_now = jnp.concatenate([carry_out, heard], axis=0)
+                opened = jnp.concatenate([heard, carry_out], 0)
+                carry_out = jnp.where(res & current_arr == 0, h_now, opened)
+                current_arr = 2 * current_arr
+            return carry_out
+
         group_one, group_two = (
-            lax.all_gather(normed_one.astype(jnp.bfloat16), "mp", axis=0, tiled=True),
+            see_routes_all(normed_one.astype(jnp.bfloat16)),
             lax.all_gather(normed_two.astype(jnp.bfloat16), "mp", axis=0, tiled=True),
         )
         plain_query_rows = jnp.dot(group_one, w_query, preferred_element_type=jnp.float32)

time: 1180 us -> 1340 us (1.14)
  waiting for transfers between devices: 617 us -> 732 us
  local copies, waits for them, and re-layouts: 104 us -> 122 us
  other arithmetic: 58.9 us -> 73.6 us
    ppermute x0 -> x6, waiting for transfers between devices: none -> 192 us  [see_routes_all(): jax.lax.ppermute(carry_out, axis_name=named_axis, perm=list(map(lambda k:...]
    all_gather x2 -> x0, waiting for transfers between devices: 83.5 us -> none  [local(): lax.all_gather(normed_one.astype(jnp.bfloat16), 'mp', axis=0, tiled=True)]
    unnamed x226 -> x243, local copies, waits for them, and re-layouts: 30.4 us -> 24 us
  transfers between devices with their start and end apart: 20 -> 24, of which waited for: 10 -> 13; matrix products, arithmetic and copies ran while one was open for 36% -> 35% of each run, Pallas kernels for 0% -> 0%
where the time goes in v1:
time: 1340 us; the launch traced here: 1330 us
  waiting for transfers between devices  732 us (55%)
  matrix products  292 us (22%)
  local copies, waits for them, and re-layouts  122 us (9%)
  other arithmetic  73.6 us (5%)
  blocking collectives  68 us (5%)
  loops' own time  18.1 us (1%)
  between operations  16.2 us (1%)
    reduce_scatter x2, waiting for transfers between devices, local(): lax.psum_scatter(jnp.dot(context_rows, w_out, preferred_element_type=jnp....  193 us
    ppermute x6, waiting for transfers between devices, see_routes_all(): jax.lax.ppermute(carry_out, axis_name=named_axis, perm=list(map(lambda k:...  192 us
    reduce_scatter x2, waiting for transfers between devices, local(): lax.psum_scatter(part_one.astype(jnp.bfloat16), 'mp', scatter_dimension=0...  154 us
    reduce_scatter x2, waiting for transfers between devices, local(): lax.psum_scatter(part_two.astype(jnp.bfloat16), 'mp', scatter_dimension=0...  153 us
    dot_general x24, matrix products, block_step(): jnp.einsum('hqk,hkd->hqd', attention_scores, value_block, precision=maxim...  58.7 us
    dot_general x24, matrix products, block_step(): jnp.einsum('ugy,uky->ugk', block_of_queries, block_of_keys, precision=max...  58 us
    psum x1, blocking collectives, local(): lax.psum((norm_sums[0], norm_sums[1], norm_sums[2], norm_sums[3]), ('seq'...  43.4 us
    dot_general x12, matrix products, contract_cols(): lax.dot_general(left_side, right_side, (((1,), (1,)), ((), ())), preferre...  33.4 us
  transfers between devices with their start and end apart: 24, of which 13 were waited for; matrix products, arithmetic and copies ran while one was open for 35% of the time, Pallas kernels for 0%

profile of v1, /device:TPU:0, one launch (start us, length us, event | category | flops | bytes accessed | tf_op | source)
XLA Modules:
  0.0 1329.5 jit_solution(10760383643183163629)
XLA Ops:
  17.8 13.2 collective-permute-done.3
  33.9 5.8 all_gather.36
  41.2 45.7 %collective-permute-done.4 = bf16[384,1024]{1,0:T(8,128)(2,1)S(1)} collective-permute-done((bf16[384,1024]{1,0:T(8,128)(2,1)S(1)}, bf16[384,1024]{1,0:T(8,128)(2,1)S(1)}, u32[]{:S(2)}, u32[]{:S(2)}) %collective-permute-start.4) | collective-permute-done | bytes 786464 | tf_op jit(solution)/shard_map/ppermute | solution.py:246
  87.7 7.2 all_gather.38
  95.0 5.8 all_gather.37
  101.0 16.1 %collective-permute-done.1 = bf16[384,1024]{1,0:T(8,128)(2,1)S(1)} collective-permute-done((bf16[384,1024]{1,0:T(8,128)(2,1)S(1)}, bf16[384,1024]{1,0:T(8,128)(2,1)S(1)}, u32[]{:S(2)}, u32[]{:S(2)}) %collective-permute-start.1) | collective-permute-done | bytes 786464 | tf_op jit(solution)/shard_map/ppermute | solution.py:246
  119.0 5.8 all_gather.39
  129.3 102.2 %collective-permute-done.5 = bf16[768,1024]{1,0:T(8,128)(2,1)} collective-permute-done((bf16[768,1024]{1,0:T(8,128)(2,1)S(1)}, bf16[768,1024]{1,0:T(8,128)(2,1)}, u32[]{:S(2)}, u32[]{:S(2)}) %collective-permute-start.5) | collective-permute-done | bytes 1572896 | tf_op jit(solution)/shard_map/ppermute | solution.py:246
  236.8 14.8 %collective-permute-done.2 = bf16[768,1024]{1,0:T(8,128)(2,1)} collective-permute-done((bf16[768,1024]{1,0:T(8,128)(2,1)}, bf16[768,1024]{1,0:T(8,128)(2,1)}, u32[]{:S(2)}, u32[]{:S(2)}) %collective-permute-start.2) | collective-permute-done | bytes 1572896 | tf_op jit(solution)/shard_map/ppermute | solution.py:246
  251.7 3.5 maximum_select_fusion
  282.1 54.4 %while.95 = (s32[]{:T(128)}, f32[2,64,64]{2,1,0:T(8,128)S(1)}, f32[2,64]{1,0:T(2,128)S(1)}, s32[]{:T(128)}, bf16[3,2,512,64]{2,3,1,0:T(8,128)(2,1)}, /*index=5*/...) while((s32[]{:T(128)}, f32[2,64,64]{2,1,0:T(8,128)S(1)}, ...), condition=%wide.region_17.18_spmd.clone, body=%wide.region_15.17_spmd.clone.sunk | while | flops 910208896 | bytes 8144617 | solution.py:176
  349.5 50.9 %while.94 = (s32[]{:T(128)}, f32[2,64,64]{2,1,0:T(8,128)S(1)}, f32[2,64]{1,0:T(2,128)S(1)}, s32[]{:T(128)}, bf16[3,2,512,64]{2,3,1,0:T(8,128)(2,1)}, /*index=5*/...) while((s32[]{:T(128)}, f32[2,64,64]{2,1,0:T(8,128)S(1)}, ...), condition=%wide.region_8.9_spmd.clone, body=%wide.region_6.8_spmd.clone.sunk | while | flops 910208896 | bytes 8145129 | solution.py:176
  410.0 76.8 %while.97 = (s32[]{:T(128)}, f32[2,64,64]{2,1,0:T(8,128)S(1)}, f32[2,64]{1,0:T(2,128)S(1)}, f32[3,2,512,64]{2,3,1,0:T(8,128)}, f32[3,2,512,64]{2,3,1,0:T(8,128)}...) while((s32[]{:T(128)}, f32[2,64,64]{2,1,0:T(8,128)S(1)}, ...), condition=%wide.region_32.33_spmd.clone, body=%wide.region_29.32_spmd.clone.sunk | while | flops 2675472384 | bytes 24581376 | solution.py:176
  494.7 3.9 fusion.248
  503.0 102.0 %while.96 = (s32[]{:T(128)}, f32[2,64,64]{2,1,0:T(8,128)}, f32[2,64]{1,0:T(2,128)}, f32[3,2,512,64]{2,3,1,0:T(8,128)}, f32[3,2,512,64]{2,3,1,0:T(8,128)}, /*inde...) while((s32[]{:T(128)}, f32[2,64,64]{2,1,0:T(8,128)}, ...), condition=%wide.region_22.23_spmd.clone, body=%wide.region_19.22_spmd.clone.sunk | while | flops 2675472384 | bytes 27727188 | solution.py:176
  634.2 12.0 multiply_convert_fusion.1
  646.2 12.1 multiply_convert_fusion
  658.4 6.2 add_convert_fusion.3
  676.1 4.3 fusion.234
  696.8 3.5 convolution_convert_fusion.1
  701.6 3.6 convolution_convert_fusion
  708.8 3.6 convolution_add_fusion.8
  715.8 3.7 convolution_add_fusion.9
  725.8 12.5 reduce-scatter.33.cloned.1.call-done
  740.1 25.4 %reduce-scatter.35.cloned.1.call-done = bf16[512,256]{1,0:T(8,128)(2,1)} async-done(((bf16[512,1024]{1,0:T(8,128)(2,1)}), bf16[512,256]{1,0:T(8,128)(2,1)}) %reduce-scatter.35.cloned.1.call-update) | async-done | bytes 262160 | tf_op jit(solution)/shard_map/reduce_scatter | solution.py:339
  767.3 76.5 %reduce-scatter.21.cloned.1.call-done = bf16[192,1024]{1,0:T(8,128)(2,1)} async-done(((bf16[1536,1024]{1,0:T(8,128)(2,1)}), bf16[192,1024]{1,0:T(8,128)(2,1)}) %reduce-scatter.21.cloned.1.call-update) | async-done | bytes 393232 | tf_op jit(solution)/shard_map/reduce_scatter | solution.py:307
  843.8 77.2 %reduce-scatter.17.cloned.1.call-done = bf16[192,1024]{1,0:T(8,128)(2,1)} async-done(((bf16[1536,1024]{1,0:T(8,128)(2,1)}), bf16[192,1024]{1,0:T(8,128)(2,1)}) %reduce-scatter.17.cloned.1.call-update) | async-done | bytes 393232 | tf_op jit(solution)/shard_map/reduce_scatter | solution.py:307
  922.7 75.7 %reduce-scatter.19.cloned.1.call-done = bf16[192,1024]{1,0:T(8,128)(2,1)} async-done(((bf16[1536,1024]{1,0:T(8,128)(2,1)}), bf16[192,1024]{1,0:T(8,128)(2,1)}) %reduce-scatter.19.cloned.1.call-update) | async-done | bytes 393232 | tf_op jit(solution)/shard_map/reduce_scatter | solution.py:310
  998.4 77.3 %reduce-scatter.23.cloned.1.call-done = bf16[192,1024]{1,0:T(8,128)(2,1)} async-done(((bf16[1536,1024]{1,0:T(8,128)(2,1)}), bf16[192,1024]{1,0:T(8,128)(2,1)}) %reduce-scatter.23.cloned.1.call-update) | async-done | bytes 393232 | tf_op jit(solution)/shard_map/reduce_scatter | solution.py:310
  1080.5 43.4 %all-reduce.12 = (f32[1024]{0:T(1024)}, f32[1024]{0:T(1024)}, f32[1024]{0:T(1024)}, f32[1024]{0:T(1024)}) all-reduce(f32[1024]{0:T(1024)S(1)} %add.341, f32[1024]{0:T(1024)S(1)} %add.342, f32[1024]{0:T(1024)S(1)} %add.343, f32[1024]{0:T(1024)S(1)} %add.344), channel_id=1, replica_groups=mesh['seq'=4,'mp'=8] {'seq','mp'}, use_global_device_ids=true, to_apply=%region_41.42 | all-reduce | flops 4096 | bytes 32768 | tf_op jit(solution)/shard_map/psum | solution.py:343
  1125.5 71.8 %reduce-scatter.15.cloned.1.call-done = f32[192,1024]{1,0:T(8,128)} async-done(((f32[1536,1024]{1,0:T(8,128)}), f32[192,1024]{1,0:T(8,128)}) %reduce-scatter.15.cloned.1.call-update) | async-done | bytes 786448 | tf_op jit(solution)/shard_map/reduce_scatter | solution.py:275
  1197.3 120.8 %reduce-scatter.13.cloned.1.call-done = f32[192,1024]{1,0:T(8,128)} async-done(((f32[1536,1024]{1,0:T(8,128)}), f32[192,1024]{1,0:T(8,128)}) %reduce-scatter.13.cloned.1.call-update) | async-done | bytes 786448 | tf_op jit(solution)/shard_map/reduce_scatter | solution.py:275
  (711 shorter events, 441.5 us)
Async XLA Ops:
  7.2 397.1 %all-gather.19.cloned.1.call-start = ((), (), s32[]{:S(2)}) async-start(), calls=%async_computation.29 | async-start | bytes 3538944 | tf_op jit(solution)/shard_map/all_gather | solution.py:283
  9.4 485.2 %all-gather.17.cloned.1.call-start = ((), (), s32[]{:S(2)}) async-start(), calls=%async_computation.28 | async-start | bytes 3538944 | tf_op jit(solution)/shard_map/all_gather | solution.py:283
  10.2 624.0 %all-gather.11.cloned.1.call-start = ((), (), s32[]{:S(2)}) async-start(), calls=%async_computation.13 | async-start | bytes 1310720 | tf_op jit(solution)/shard_map/all_gather | solution.py:232
  10.9 623.3 %all-gather.9.cloned.1.call-start = ((), (), s32[]{:S(2)}) async-start(), calls=%async_computation.12 | async-start | bytes 3538944 | tf_op jit(solution)/shard_map/all_gather | solution.py:259
  13.6 632.6 %all-gather.15.cloned.1.call-start = ((), (), s32[]{:S(2)}) async-start(), calls=%async_computation.16 | async-start | bytes 3538944 | tf_op jit(solution)/shard_map/all_gather | solution.py:259
  14.1 644.2 %all-gather.13.cloned.1.call-start = ((), (), s32[]{:S(2)}) async-start(), calls=%async_computation.14 | async-start | bytes 1310720 | tf_op jit(solution)/shard_map/all_gather | solution.py:233
  14.2 16.8 %collective-permute-start.3 = (bf16[192,1024]{1,0:T(8,128)(2,1)S(1)}, bf16[192,1024]{1,0:T(8,128)(2,1)S(1)}, u32[]{:S(2)}, u32[]{:S(2)}) collective-permute-start(bf16[192,1024]{1,0:T(8,128)(2,1)S(1)} %get-tuple-element.1358), channel_id=1, source_target_pairs={{0,1},{1,0},{2,3},{3,2},{4,5},{5,4},{6,7},{7,6},{8,9},{9,8},{10,11... | collective-permute-start | bytes 1179656 | tf_op jit(solution)/shard_map/ppermute | solution.py:246
  17.3 22.5 %collective-permute-start = (bf16[192,1024]{1,0:T(8,128)(2,1)S(1)}, bf16[192,1024]{1,0:T(8,128)(2,1)S(1)}, u32[]{:S(2)}, u32[]{:S(2)}) collective-permute-start(bf16[192,1024]{1,0:T(8,128)(2,1)S(1)} %get-tuple-element.1359), channel_id=1, source_target_pairs={{0,1},{1,0},{2,3},{3,2},{4,5},{5,4},{6,7},{7,6},{8,9},{9,8},{10,11... | collective-permute-start | bytes 1179656 | tf_op jit(solution)/shard_map/ppermute | solution.py:246
  17.4 702.3 %reduce-scatter.29.cloned.1.call-start = ((), (), s32[]{:S(2)}) async-start(), calls=%async_computation.24 | async-start | bytes 327680 | tf_op jit(solution)/shard_map/reduce_scatter | solution.py:330
  31.3 55.7 %collective-permute-start.4 = (bf16[384,1024]{1,0:T(8,128)(2,1)S(1)}, bf16[384,1024]{1,0:T(8,128)(2,1)S(1)}, u32[]{:S(2)}, u32[]{:S(2)}) collective-permute-start(bf16[384,1024]{1,0:T(8,128)(2,1)S(1)} %maximum_select_fusion.5), channel_id=1, source_target_pairs={{0,2},{1,3},{2,0},{3,1},{4,6},{5,7},{6,4},{7,5},{8,10},{9,11},{10,... | collective-permute-start | bytes 2359304 | tf_op jit(solution)/shard_map/ppermute | solution.py:246
  39.7 217.6 %copy-start.25 = (bf16[1024,128]{1,0:T(8,128)(2,1)}, bf16[1024,128]{1,0:T(8,128)(2,1)S(1)}, u32[]{:S(2)}) copy-start(bf16[1024,128]{1,0:T(8,128)(2,1)S(1)} %all_gather.36) | copy-start | bytes 786436
  40.1 77.0 %collective-permute-start.1 = (bf16[384,1024]{1,0:T(8,128)(2,1)S(1)}, bf16[384,1024]{1,0:T(8,128)(2,1)S(1)}, u32[]{:S(2)}, u32[]{:S(2)}) collective-permute-start(bf16[384,1024]{1,0:T(8,128)(2,1)S(1)} %maximum_select_fusion.4), channel_id=1, source_target_pairs={{0,2},{1,3},{2,0},{3,1},{4,6},{5,7},{6,4},{7,5},{8,10},{9,11},{10,... | collective-permute-start | bytes 2359304 | tf_op jit(solution)/shard_map/ppermute | solution.py:246
  87.6 143.8 %collective-permute-start.5 = (bf16[768,1024]{1,0:T(8,128)(2,1)S(1)}, bf16[768,1024]{1,0:T(8,128)(2,1)}, u32[]{:S(2)}, u32[]{:S(2)}) collective-permute-start(bf16[768,1024]{1,0:T(8,128)(2,1)S(1)} %maximum_select_fusion.3), channel_id=1, source_target_pairs={{0,4},{1,5},{2,6},{3,7},{4,0},{5,1},{6,2},{7,3},{8,12},{9,13},{10,... | collective-permute-start | bytes 4718600 | tf_op jit(solution)/shard_map/ppermute | solution.py:246
  118.9 132.7 %collective-permute-start.2 = (bf16[768,1024]{1,0:T(8,128)(2,1)}, bf16[768,1024]{1,0:T(8,128)(2,1)}, u32[]{:S(2)}, u32[]{:S(2)}) collective-permute-start(bf16[768,1024]{1,0:T(8,128)(2,1)} %maximum_select_fusion.2), channel_id=1, source_target_pairs={{0,4},{1,5},{2,6},{3,7},{4,0},{5,1},{6,2},{7,3},{8,12},{9,13},{10,... | collective-permute-start | bytes 4718600 | tf_op jit(solution)/shard_map/ppermute | solution.py:246
  124.7 369.9 %copy-start.23 = (bf16[128,1024]{1,0:T(8,128)(2,1)}, bf16[128,1024]{1,0:T(8,128)(2,1)S(1)}, u32[]{:S(2)}) copy-start(bf16[128,1024]{1,0:T(8,128)(2,1)S(1)} %all_gather.39) | copy-start | bytes 786436
  620.3 100.9 %reduce-scatter.27.cloned.1.call-start = ((), (), s32[]{:S(2)}) async-start(), calls=%async_computation.23 | async-start | bytes 327680 | tf_op jit(solution)/shard_map/reduce_scatter | solution.py:327
  625.1 97.7 %reduce-scatter.25.cloned.1.call-start = ((), (), s32[]{:S(2)}) async-start(), calls=%async_computation.22 | async-start | bytes 327680 | tf_op jit(solution)/shard_map/reduce_scatter | solution.py:324
  629.8 94.5 %reduce-scatter.31.cloned.1.call-start = ((), (), s32[]{:S(2)}) async-start(), calls=%async_computation.25 | async-start | bytes 327680 | tf_op jit(solution)/shard_map/reduce_scatter | solution.py:333
  634.1 104.2 %reduce-scatter.33.cloned.1.call-start = ((), (), s32[]{:S(2)}) async-start(), calls=%async_computation.26 | async-start | bytes 1310720 | tf_op jit(solution)/shard_map/reduce_scatter | solution.py:336
  676.1 89.4 %reduce-scatter.35.cloned.1.call-start = ((), (), s32[]{:S(2)}) async-start(), calls=%async_computation.27 | async-start | bytes 1310720 | tf_op jit(solution)/shard_map/reduce_scatter | solution.py:339
  683.3 160.5 %reduce-scatter.21.cloned.1.call-start = ((), (), s32[]{:S(2)}) async-start(), calls=%async_computation.20 | async-start | bytes 3538944 | tf_op jit(solution)/shard_map/reduce_scatter | solution.py:307
  689.3 231.8 %reduce-scatter.17.cloned.1.call-start = ((), (), s32[]{:S(2)}) async-start(), calls=%async_computation.18 | async-start | bytes 3538944 | tf_op jit(solution)/shard_map/reduce_scatter | solution.py:307
  695.0 303.4 %reduce-scatter.19.cloned.1.call-start = ((), (), s32[]{:S(2)}) async-start(), calls=%async_computation.19 | async-start | bytes 3538944 | tf_op jit(solution)/shard_map/reduce_scatter | solution.py:310
  700.2 375.4 %reduce-scatter.23.cloned.1.call-start = ((), (), s32[]{:S(2)}) async-start(), calls=%async_computation.21 | async-start | bytes 3538944 | tf_op jit(solution)/shard_map/reduce_scatter | solution.py:310
  705.2 492.0 %reduce-scatter.15.cloned.1.call-start = ((), (), s32[]{:S(2)}) async-start(), calls=%async_computation.17 | async-start | bytes 7077888 | tf_op jit(solution)/shard_map/reduce_scatter | solution.py:275
  712.5 605.5 %reduce-scatter.13.cloned.1.call-start = ((), (), s32[]{:S(2)}) async-start(), calls=%async_computation.15 | async-start | bytes 7077888 | tf_op jit(solution)/shard_map/reduce_scatter | solution.py:275
  719.6 356.1 %copy-start.80 = (f32[1024]{0:T(1024)S(1)}, f32[1024]{0:T(1024)}, u32[]{:S(2)}) copy-start(f32[1024]{0:T(1024)} %param.26) | copy-start | bytes 12292
  719.6 356.1 %copy-start.92 = (f32[192]{0:T(256)S(1)}, f32[192]{0:T(256)}, u32[]{:S(2)}) copy-start(f32[192]{0:T(256)} %copy-done.91) | copy-start | bytes 2308
  719.6 356.1 %copy-start.96 = (f32[192]{0:T(256)S(1)}, f32[192]{0:T(256)}, u32[]{:S(2)}) copy-start(f32[192]{0:T(256)} %copy-done.95) | copy-start | bytes 2308
  843.8 280.1 %copy-start.41 = (bf16[192,1024]{1,0:T(8,128)(2,1)S(1)}, bf16[192,1024]{1,0:T(8,128)(2,1)}, u32[]{:S(2)}) copy-start(bf16[192,1024]{1,0:T(8,128)(2,1)} %reduce-scatter.21.cloned.1.call-done) | copy-start | bytes 1179652
  1075.7 242.4 %copy-start.43 = (bf16[192,1024]{1,0:T(8,128)(2,1)S(1)}, bf16[192,1024]{1,0:T(8,128)(2,1)}, u32[]{:S(2)}) copy-start(bf16[192,1024]{1,0:T(8,128)(2,1)} %reduce-scatter.17.cloned.1.call-done) | copy-start | bytes 1179652
  1075.7 242.4 %copy-start.44 = (bf16[192,1024]{1,0:T(8,128)(2,1)S(1)}, bf16[192,1024]{1,0:T(8,128)(2,1)}, u32[]{:S(2)}) copy-start(bf16[192,1024]{1,0:T(8,128)(2,1)} %reduce-scatter.19.cloned.1.call-done) | copy-start | bytes 1179652
  (120 other events, 2866.0 us)
Sparse Core Ops, SparseCore 0:
  10.2 100.8 all-gather.18
  113.3 117.6 all-gather.16
  232.5 15.5 all-gather.10
  250.1 60.0 all-gather.8
  312.2 58.9 all-gather.14
  372.6 15.3 all-gather.12
  620.5 22.3 reduce-scatter.28
  645.3 20.0 reduce-scatter.26
  667.8 20.0 reduce-scatter.24
  690.8 20.0 reduce-scatter.30
  713.5 24.8 reduce-scatter.32
  740.7 24.7 reduce-scatter.34
  769.1 74.6 reduce-scatter.20
  847.3 73.7 reduce-scatter.16
  924.5 73.8 reduce-scatter.18
  1001.8 73.7 reduce-scatter.22
  1079.1 118.1 reduce-scatter.14
  1200.7 117.2 reduce-scatter.12
